TPU v7x, 32 devices: a whole 2x2x4 slice. The times are simulated.
32 devices in a mesh: dp: 8 (over y, x, core), fsdp: 4 (over z).
Axes of the slice: x: 2, y: 2, z: 4, core: 2. Of those that a mesh axis runs over, the one named last changes fastest.
Arguments:
- gradients: bfloat16 [8, 512, 8192], P('dp', None, 'fsdp'), may hold values from -1.5 to 1.5
- momentum: float32 [512, 8192], P('dp', 'fsdp'), may hold values from -1500 to 1500
- weight: float32 [512, 8192], P(None, 'fsdp'), may hold values from -3 to 3
- logit_peaks: int32 [32, 32], P(('dp', 'fsdp')), may hold values from 0 to 479, as said below
- clip_threshold: int32 [1], replicated, may hold values from 60 to 120
Outputs:
- new_weight: float32 [512, 8192], P(None, 'fsdp')
- new_momentum: float32 [512, 8192], P('dp', 'fsdp')
- update_norm: float32 [1], replicated
Inputs may be any that keep to these rules, and one draw needn't show every extreme that they name: `logit_peaks`: for every head, the largest entry over all rows is at least 40.
All inputs are finite; a program needn't handle non-finite values.
Results may differ from a plain program's by a relative error of at most 0.0023.
Values may be sent and summed in bfloat16 or wider, within the bound.
A program may use at most 64 MiB of HBM per device.

v0:
```python
import math
import jax
import jax.numpy as jnp
from jax import lax
from jax.sharding import PartitionSpec as P

KVL = 512
NOPE = 128
VDIM = 128
HEADS = 32
ITERS = 3
KVO = 8192
quintic_terms = (3.4445, -4.775, 2.0315)
learning_rate = 0.5
weight_decay = 0.1
momentum_decay = 0.95
update_gain = 0.2
epsilon = 1e-07


def column_factors(global_peaks, clip_threshold):
    largest = jnp.max(global_peaks, axis=0).astype(jnp.float32)
    clip_ratio = jnp.minimum(1.0, clip_threshold.astype(jnp.float32)[0] / largest)
    key_scale = jnp.sqrt(clip_ratio)
    per_head = jnp.concatenate(
        [jnp.broadcast_to(key_scale[:, None], (HEADS, NOPE)), jnp.ones((HEADS, VDIM), jnp.float32)],
        axis=1,
    )
    return per_head.reshape(HEADS * (NOPE + VDIM))


def gram_over_replicas(partial_gram):
    return lax.psum(partial_gram.astype(jnp.bfloat16), "dp").astype(jnp.float32)


def newton_schulz(column_block, gram_sum):
    current = column_block
    for iteration in range(ITERS):
        partial_gram = lax.dot_general(
            current,
            current,
            (((1,), (1,)), ((), ())),
            precision=lax.Precision.HIGHEST,
            preferred_element_type=jnp.float32,
        )
        square = gram_sum(partial_gram)
        combined = quintic_terms[1] * square + quintic_terms[2] * jnp.dot(
            square, square, precision=lax.Precision.HIGHEST, preferred_element_type=jnp.float32
        )
        current = quintic_terms[0] * current + jnp.dot(
            combined, current, precision=lax.Precision.HIGHEST, preferred_element_type=jnp.float32
        )
    return current


def local(gradients, momentum, weight, logit_peaks, clip_threshold):
    replica_shard = gradients[0].astype(jnp.float32)
    summed = lax.psum_scatter(
        replica_shard.astype(jnp.bfloat16), "dp", scatter_dimension=0, tiled=True
    ).astype(jnp.float32)
    new_momentum = momentum_decay * momentum + summed
    blended = summed + momentum_decay * new_momentum
    global_peaks = lax.pmax(logit_peaks, ("dp", "fsdp"))
    square_total = lax.psum(jnp.sum(blended * blended), ("dp", "fsdp"))
    update_norm = jnp.sqrt(square_total / (KVL * KVO)).reshape(1)
    normalized = blended / (jnp.sqrt(square_total) + epsilon)
    dp_count = lax.axis_size("dp")
    fsdp_count = lax.axis_size("fsdp")
    row_count = normalized.shape[0]
    shard_cols = normalized.shape[1]
    piece_cols = shard_cols // dp_count
    wide_rows = lax.all_gather(normalized.astype(jnp.bfloat16), "fsdp", axis=1, tiled=True).astype(
        normalized.dtype
    )
    split_up = wide_rows.reshape(row_count, fsdp_count, dp_count, piece_cols)
    columns = lax.all_to_all(
        split_up.astype(jnp.bfloat16), "dp", split_axis=2, concat_axis=0, tiled=True
    ).astype(split_up.dtype)
    column_block = columns.reshape(KVL, fsdp_count * piece_cols)
    orthogonal = newton_schulz(column_block, gram_over_replicas)
    orthogonal_all = orthogonal.reshape(KVL, fsdp_count, piece_cols)
    own_block = lax.dynamic_index_in_dim(orthogonal_all, lax.axis_index("fsdp"), 1, keepdims=False)
    shard_orthogonal = lax.all_gather(
        own_block.astype(jnp.bfloat16), "dp", axis=1, tiled=True
    ).astype(own_block.dtype)
    update_scale = update_gain * math.sqrt(max(KVL, KVO))
    stepped = weight - learning_rate * (update_scale * shard_orthogonal + weight_decay * weight)
    factors = column_factors(global_peaks, clip_threshold)
    shard_factors = lax.dynamic_slice_in_dim(
        factors, lax.axis_index("fsdp") * shard_cols, shard_cols
    )
    new_weight = stepped * shard_factors[None, :]
    return (new_weight, new_momentum, update_norm)


def solution(mesh):
    placed = (P("dp", None, "fsdp"), P("dp", "fsdp"), P(None, "fsdp"), P(("dp", "fsdp"), None), P())
    return jax.shard_map(
        local,
        mesh=mesh,
        in_specs=placed,
        out_specs=(P(None, "fsdp"), P("dp", "fsdp"), P()),
        check_vma=False,
    )
```

profile of v0, /device:TPU:0, one launch (start us, length us, event | category | flops | bytes accessed | tf_op | source)
XLA Modules:
  0.0 393.2 jit_solution(4246581110344312407)
XLA Ops:
  8.0 47.2 %reduce-scatter.2.cloned.1.call-done = bf16[64,2048]{1,0:T(8,128)(2,1)} async-done(((bf16[512,2048]{1,0:T(8,128)(2,1)}), bf16[64,2048]{1,0:T(8,128)(2,1)}) %reduce-scatter.2.cloned.1.call-update) | async-done | bytes 262160 | tf_op jit(solution)/shard_map/reduce_scatter | solution.py:58
  55.1 1.7 multiply_reduce_fusion
  56.8 39.5 %psum.28 = f32[]{:T(128)} all-reduce(f32[]{:T(128)} %get-tuple-element.3), channel_id=1, replica_groups=mesh['dp'=8,'fsdp'=4] {'dp','fsdp'}, use_global_device_ids=true, to_apply=%region_2.0 | all-reduce | flops 1 | bytes 8 | tf_op jit(solution)/shard_map/psum | solution.py:64
  97.0 1.7 divide_convert_fusion
  98.8 29.1 %all-gather.4.cloned.1.call-done = bf16[64,8192]{1,0:T(8,128)(2,1)} async-done(((bf16[64,2048]{1,0:T(8,128)(2,1)}), bf16[64,8192]{1,0:T(8,128)(2,1)}) %all-gather.4.cloned.1.call-update) | async-done | bytes 1048592 | tf_op jit(solution)/shard_map/all_gather | solution.py:72
  127.9 1.5 copy.11
  129.8 18.8 %all_to_all.18 = bf16[64,4,8,256]{3,1,0,2:T(4,128)(2,1)S(1)} all-to-all(bf16[64,4,8,256]{3,1,0,2:T(4,128)(2,1)S(1)} %copy.8), channel_id=1, replica_groups=mesh['dp'=8,'fsdp'=4] {'dp'}, dimensions={2} | all-to-all | bytes 2097152 | tf_op jit(solution)/shard_map/all_to_all | solution.py:76
  148.8 1.5 convolution_convert_fusion.2
  150.4 52.5 %all-reduce.5.cloned.1.call-done = bf16[512,512]{1,0:T(8,128)(2,1)} async-done(((bf16[512,512]{1,0:T(8,128)(2,1)}), bf16[512,512]{1,0:T(8,128)(2,1)}) %all-reduce.5.cloned.1.call-update) | async-done | bytes 524304 | tf_op jit(solution)/shard_map/psum | solution.py:33
  202.9 1.9 fusion.5
  204.8 1.8 multiply_add_fusion.2
  206.6 1.3 copy-done
  207.9 4.3 %convolution_convert_fusion.1 = bf16[512,512]{1,0:T(8,128)(2,1)} fusion(f32[512,1024]{1,0:T(8,128)S(1)} %multiply_add_fusion.2), kind=kOutput, calls=%fused_computation.14 | convolution fusion | flops 3221487616 | bytes 2621440 | tf_op jit(solution)/shard_map/dot_general | solution.py:39
  212.5 54.0 %all-reduce.7.cloned.1.call-done = bf16[512,512]{1,0:T(8,128)(2,1)} async-done(((bf16[512,512]{1,0:T(8,128)(2,1)}), bf16[512,512]{1,0:T(8,128)(2,1)}) %all-reduce.7.cloned.1.call-update) | async-done | bytes 524304 | tf_op jit(solution)/shard_map/psum | solution.py:33
  266.5 1.9 fusion.4
  268.6 3.7 multiply_add_fusion.1
  272.2 4.3 %convolution_convert_fusion = bf16[512,512]{1,0:T(8,128)(2,1)} fusion(f32[512,1024]{1,0:T(8,128)S(1)} %multiply_add_fusion.1), kind=kOutput, calls=%fused_computation.13 | convolution fusion | flops 3221487616 | bytes 2621440 | tf_op jit(solution)/shard_map/dot_general | solution.py:39
  276.6 54.2 %all-reduce.9.cloned.1.call-done = bf16[512,512]{1,0:T(8,128)(2,1)} async-done(((bf16[512,512]{1,0:T(8,128)(2,1)}), bf16[512,512]{1,0:T(8,128)(2,1)}) %all-reduce.9.cloned.1.call-update) | async-done | bytes 524304 | tf_op jit(solution)/shard_map/psum | solution.py:33
  330.9 1.9 fusion.3
  332.8 3.6 multiply_add_fusion
  336.4 0.8 reshape.40
  337.7 0.7 copy.15
  338.5 39.3 %pmax.7 = s32[1,32]{1,0:T(1,128)S(1)} all-reduce(s32[1,32]{1,0:T(1,128)S(1)} %copy-done.4), channel_id=1, replica_groups=mesh['dp'=8,'fsdp'=4] {'dp','fsdp'}, use_global_device_ids=true, to_apply=%region_6.0 | all-reduce | flops 32 | bytes 256 | tf_op jit(solution)/shard_map/pmax | solution.py:63
  379.3 5.9 %fusion.2 = f32[512,2048]{1,0:T(8,128)} fusion(f32[512,2048]{1,0:T(8,128)} %param.7, bf16[512,1,2048]{2,0,1:T(8,128)(2,1)} %all-gather.6.cloned.1.call-done, f32[2048]{0:T(1024)S(1)} %dynamic_slice.8), kind=kLoop, calls=%fused_computation.3 | loop fusion | flops 7340032 | bytes 10493952 | tf_op jit(solution)/shard_map/mul | solution.py:92
  (30 shorter events, 2.6 us)
Async XLA Ops:
  7.2 48.0 %copy-start.3 = (f32[64,2048]{1,0:T(8,128)S(1)}, f32[64,2048]{1,0:T(8,128)}, u32[]{:S(2)}) copy-start(f32[64,2048]{1,0:T(8,128)} %param.6) | copy-start | bytes 1572868
  7.2 48.0 %reduce-scatter.2.cloned.1.call-start = ((), (), s32[]{:S(2)}) async-start(), calls=%async_computation.2 | async-start | bytes 2359296 | tf_op jit(solution)/shard_map/reduce_scatter | solution.py:58
  7.9 120.0 %all-gather.4.cloned.1.call-start = ((), (), s32[]{:S(2)}) async-start(), calls=%async_computation.3 | async-start | bytes 1310720 | tf_op jit(solution)/shard_map/all_gather | solution.py:72
  56.8 72.9 %copy-start.2 = (f32[64,2048]{1,0:T(8,128)}, f32[64,2048]{1,0:T(8,128)S(1)}, u32[]{:S(2)}) copy-start(f32[64,2048]{1,0:T(8,128)S(1)} %get-tuple-element.4) | copy-start | bytes 1572868
  98.7 104.1 %all-reduce.5.cloned.1.call-start = ((), (), s32[]{:S(2)}) async-start(), calls=%async_computation.4 | async-start | bytes 1048576 | tf_op jit(solution)/shard_map/psum | solution.py:33
  150.3 116.2 %all-reduce.7.cloned.1.call-start = ((), (), s32[]{:S(2)}) async-start(), calls=%async_computation.5 | async-start | bytes 1048576 | tf_op jit(solution)/shard_map/psum | solution.py:33
  206.6 1.3 copy-start
  212.3 118.6 %all-reduce.9.cloned.1.call-start = ((), (), s32[]{:S(2)}) async-start(), calls=%async_computation.6 | async-start | bytes 1048576 | tf_op jit(solution)/shard_map/psum | solution.py:33
  266.5 2.1 copy-start.1
  276.6 102.7 %all-gather.6.cloned.1.call-start = ((), (), s32[]{:S(2)}) async-start(), calls=%async_computation.7 | async-start | bytes 2359296 | tf_op jit(solution)/shard_map/all_gather | solution.py:83
  336.4 2.1 copy-start.4
Sparse Core Ops, SparseCore 0:
  11.3 43.8 reduce-scatter.1
  98.9 28.9 all-gather.3
  150.5 52.3 all-reduce.4
  212.4 54.0 all-reduce.6
  276.7 54.1 all-reduce.8
  338.6 27.4 all-gather.5
where the time goes:
time: 394 us; the launch traced here: 393 us
  waiting for transfers between devices  238 us (60%)
  blocking collectives  97.5 us (25%)
  matrix products  25 us (6%)
  between operations  17.4 us (4%)
  other arithmetic  9.38 us (2%)
  local copies, waits for them, and re-layouts  5.74 us (1%)
    psum x3, waiting for transfers between devices, gram_over_replicas(): return lax.psum(partial_gram.astype(jnp.bfloat16), 'dp').astype(jnp.float32)  161 us
    reduce_scatter x1, waiting for transfers between devices, local(): lax.psum_scatter(replica_shard.astype(jnp.bfloat16), 'dp', scatter_dimens...  47.2 us
    psum x1, blocking collectives, local(): square_total = lax.psum(jnp.sum(blended * blended), ('dp', 'fsdp'))  39.5 us
    pmax x1, blocking collectives, local(): global_peaks = lax.pmax(logit_peaks, ('dp', 'fsdp'))  39.3 us
    all_gather x1, waiting for transfers between devices, local(): lax.all_gather(normalized.astype(jnp.bfloat16), 'fsdp', axis=1, tiled=True)  29.1 us
    all_to_all x1, blocking collectives, local(): lax.all_to_all(split_up.astype(jnp.bfloat16), 'dp', split_axis=2, concat_...  18.8 us
    dot_general x3, matrix products, newton_schulz(): lax.dot_general(current, current, (((1,), (1,)), ((), ())), precision=lax...  10.2 us
    dot_general x3, matrix products, newton_schulz(): jnp.dot(combined, current, precision=lax.Precision.HIGHEST, preferred_ele...  9.1 us
  transfers between devices with their start and end apart: 6, of which 5 were waited for; matrix products, arithmetic and copies ran while one was open for 0% of the time, Pallas kernels for 0%

commit v1 on v0

--- a/solution.py
+++ b/solution.py
@@ -30,7 +30,9 @@
 
 
 def gram_over_replicas(partial_gram):
-    return lax.psum(partial_gram.astype(jnp.bfloat16), "dp").astype(jnp.float32)
+    return jnp.sum(lax.all_gather(partial_gram.astype(jnp.bfloat16), "dp"), axis=0).astype(
+        jnp.float32
+    )
 
 
 def newton_schulz(column_block, gram_sum):

time: 394 us -> 346 us (0.88)
  waiting for transfers between devices: 238 us -> 184 us
  other arithmetic: 9.38 us -> 18.5 us
  matrix products: 25 us -> 20.6 us
    psum x3 -> x0, waiting for transfers between devices: 161 us -> none  [gram_over_replicas(): return lax.psum(partial_gram.astype(jnp.bfloat16), 'dp').astype(jnp.float32)]
    all_gather x0 -> x3, waiting for transfers between devices: none -> 107 us  [gram_over_replicas(): lax.all_gather(partial_gram.astype(jnp.bfloat16), 'dp')]
    reduce_sum x0 -> x3, other arithmetic: none -> 9.17 us  [gram_over_replicas(): jnp.sum(lax.all_gather(partial_gram.astype(jnp.bfloat16), 'dp'), axis=0)]
    dot_general x3, matrix products: 5.7 us -> 1.3 us  [newton_schulz(): jnp.dot(square, square, precision=lax.Precision.HIGHEST, preferred_elemen...]
where the time goes in v1:
time: 346 us
  waiting for transfers between devices  184 us (53%)
  blocking collectives  97.6 us (28%)
  matrix products  20.6 us (6%)
  other arithmetic  18.5 us (5%)
  between operations  17.5 us (5%)
  local copies, waits for them, and re-layouts  6.77 us (2%)
    all_gather x3, waiting for transfers between devices, gram_over_replicas(): lax.all_gather(partial_gram.astype(jnp.bfloat16), 'dp')  107 us
    reduce_scatter x1, waiting for transfers between devices, local(): lax.psum_scatter(replica_shard.astype(jnp.bfloat16), 'dp', scatter_dimens...  47.2 us
    psum x1, blocking collectives, local(): square_total = lax.psum(jnp.sum(blended * blended), ('dp', 'fsdp'))  39.5 us
    pmax x1, blocking collectives, local(): global_peaks = lax.pmax(logit_peaks, ('dp', 'fsdp'))  39.4 us
    all_gather x1, waiting for transfers between devices, local(): lax.all_gather(normalized.astype(jnp.bfloat16), 'fsdp', axis=1, tiled=True)  29.1 us
    all_to_all x1, blocking collectives, local(): lax.all_to_all(split_up.astype(jnp.bfloat16), 'dp', split_axis=2, concat_...  18.8 us
    dot_general x3, matrix products, newton_schulz(): lax.dot_general(current, current, (((1,), (1,)), ((), ())), precision=lax...  10.2 us
    reduce_sum x3, other arithmetic, gram_over_replicas(): jnp.sum(lax.all_gather(partial_gram.astype(jnp.bfloat16), 'dp'), axis=0)  9.17 us
  transfers between devices with their start and end apart: 6, of which 5 were waited for; matrix products, arithmetic and copies ran while one was open for 0% of the time, Pallas kernels for 0%

profile of v1, /device:TPU:0, one launch (start us, length us, event | category | flops | bytes accessed | tf_op | source)
XLA Modules:
  0.0 345.9 jit_solution(12184027605742117671)
XLA Ops:
  8.0 47.2 %reduce-scatter.2.cloned.1.call-done = bf16[64,2048]{1,0:T(8,128)(2,1)} async-done(((bf16[512,2048]{1,0:T(8,128)(2,1)}), bf16[64,2048]{1,0:T(8,128)(2,1)}) %reduce-scatter.2.cloned.1.call-update) | async-done | bytes 262160 | tf_op jit(solution)/shard_map/reduce_scatter | solution.py:60
  55.1 1.7 multiply_reduce_fusion
  56.8 39.5 %psum.7 = f32[]{:T(128)} all-reduce(f32[]{:T(128)} %get-tuple-element.3), channel_id=1, replica_groups=mesh['dp'=8,'fsdp'=4] {'dp','fsdp'}, use_global_device_ids=true, to_apply=%region_2.0 | all-reduce | flops 1 | bytes 8 | tf_op jit(solution)/shard_map/psum | solution.py:66
  97.0 1.7 divide_convert_fusion
  98.8 29.1 %all-gather.10.cloned.1.call-done = bf16[64,8192]{1,0:T(8,128)(2,1)} async-done(((bf16[64,2048]{1,0:T(8,128)(2,1)}), bf16[64,8192]{1,0:T(8,128)(2,1)}) %all-gather.10.cloned.1.call-update) | async-done | bytes 1048592 | tf_op jit(solution)/shard_map/all_gather | solution.py:74
  127.9 1.5 copy.11
  129.8 18.8 %all_to_all.18 = bf16[64,4,8,256]{3,1,0,2:T(4,128)(2,1)S(1)} all-to-all(bf16[64,4,8,256]{3,1,0,2:T(4,128)(2,1)S(1)} %copy.8), channel_id=1, replica_groups=mesh['dp'=8,'fsdp'=4] {'dp'}, dimensions={2} | all-to-all | bytes 2097152 | tf_op jit(solution)/shard_map/all_to_all | solution.py:78
  148.8 1.5 convolution_convert_fusion.2
  150.4 34.2 %all-gather.12.cloned.1.call-done = bf16[4096,512]{1,0:T(8,128)(2,1)} async-done(((bf16[512,512]{1,0:T(8,128)(2,1)}), bf16[4096,512]{1,0:T(8,128)(2,1)}) %all-gather.12.cloned.1.call-update) | async-done | bytes 4194320 | tf_op jit(solution)/shard_map/all_gather | solution.py:33
  184.6 3.1 reduce_sum.46
  188.1 1.8 multiply_add_fusion.2
  190.0 1.3 copy-done
  191.3 4.3 %convolution_convert_fusion.1 = bf16[512,512]{1,0:T(8,128)(2,1)} fusion(f32[512,1024]{1,0:T(8,128)S(1)} %multiply_add_fusion.2), kind=kOutput, calls=%fused_computation.14 | convolution fusion | flops 3221487616 | bytes 2621440 | tf_op jit(solution)/shard_map/dot_general | solution.py:41
  195.9 36.5 %all-gather.14.cloned.1.call-done = bf16[4096,512]{1,0:T(8,128)(2,1)} async-done(((bf16[512,512]{1,0:T(8,128)(2,1)}), bf16[4096,512]{1,0:T(8,128)(2,1)}) %all-gather.14.cloned.1.call-update) | async-done | bytes 4194320 | tf_op jit(solution)/shard_map/all_gather | solution.py:33
  232.4 3.1 reduce_sum.47
  235.9 1.1 copy-done.1
  237.1 3.7 %multiply_add_fusion.1 = f32[512,1024]{1,0:T(8,128)S(1)} fusion(f32[512,1024]{1,0:T(8,128)S(1)} %copy-done.1, f32[512,512]{1,0:T(8,128)S(1)} %fusion.4), kind=kOutput, calls=%fused_computation.5 | convolution fusion | flops 3222274048 | bytes 5242880 | tf_op jit(solution)/shard_map/dot_general | solution.py:52
  240.7 4.3 %convolution_convert_fusion = bf16[512,512]{1,0:T(8,128)(2,1)} fusion(f32[512,1024]{1,0:T(8,128)S(1)} %multiply_add_fusion.1), kind=kOutput, calls=%fused_computation.13 | convolution fusion | flops 3221487616 | bytes 2621440 | tf_op jit(solution)/shard_map/dot_general | solution.py:41
  245.4 36.5 %all-gather.16.cloned.1.call-done = bf16[4096,512]{1,0:T(8,128)(2,1)} async-done(((bf16[512,512]{1,0:T(8,128)(2,1)}), bf16[4096,512]{1,0:T(8,128)(2,1)}) %all-gather.16.cloned.1.call-update) | async-done | bytes 4194320 | tf_op jit(solution)/shard_map/all_gather | solution.py:33
  281.8 3.1 reduce_sum.48
  285.3 3.6 %multiply_add_fusion = bf16[512,1024]{1,0:T(8,128)(2,1)S(1)} fusion(f32[512,1024]{1,0:T(8,128)S(1)} %multiply_add_fusion.1, f32[512,512]{1,0:T(8,128)S(1)} %fusion.3), kind=kOutput, calls=%fused_computation.4 | convolution fusion | flops 3222798336 | bytes 4194304 | tf_op jit(solution)/shard_map/dot_general | solution.py:52
  288.9 0.8 reshape.40
  291.1 39.4 %pmax.7 = s32[1,32]{1,0:T(1,128)S(1)} all-reduce(s32[1,32]{1,0:T(1,128)S(1)} %copy-done.4), channel_id=1, replica_groups=mesh['dp'=8,'fsdp'=4] {'dp','fsdp'}, use_global_device_ids=true, to_apply=%region_6.0 | all-reduce | flops 32 | bytes 256 | tf_op jit(solution)/shard_map/pmax | solution.py:65
  332.0 5.9 %fusion.2 = f32[512,2048]{1,0:T(8,128)} fusion(f32[512,2048]{1,0:T(8,128)} %param.7, bf16[512,1,2048]{2,0,1:T(8,128)(2,1)} %all-gather.18.cloned.1.call-done, f32[2048]{0:T(1024)S(1)} %dynamic_slice.8), kind=kLoop, calls=%fused_computation.3 | loop fusion | flops 7340032 | bytes 10493952 | tf_op jit(solution)/shard_map/mul | solution.py:94
  (33 shorter events, 4.8 us)
Async XLA Ops:
  7.2 48.0 %copy-start.3 = (f32[64,2048]{1,0:T(8,128)S(1)}, f32[64,2048]{1,0:T(8,128)}, u32[]{:S(2)}) copy-start(f32[64,2048]{1,0:T(8,128)} %param.6) | copy-start | bytes 1572868
  7.2 48.0 %reduce-scatter.2.cloned.1.call-start = ((), (), s32[]{:S(2)}) async-start(), calls=%async_computation.2 | async-start | bytes 2359296 | tf_op jit(solution)/shard_map/reduce_scatter | solution.py:60
  7.9 119.9 %all-gather.10.cloned.1.call-start = ((), (), s32[]{:S(2)}) async-start(), calls=%async_computation.3 | async-start | bytes 1310720 | tf_op jit(solution)/shard_map/all_gather | solution.py:74
  56.8 72.9 %copy-start.2 = (f32[64,2048]{1,0:T(8,128)}, f32[64,2048]{1,0:T(8,128)S(1)}, u32[]{:S(2)}) copy-start(f32[64,2048]{1,0:T(8,128)S(1)} %get-tuple-element.4) | copy-start | bytes 1572868
  98.7 85.9 %all-gather.12.cloned.1.call-start = ((), (), s32[]{:S(2)}) async-start(), calls=%async_computation.4 | async-start | bytes 4718592 | tf_op jit(solution)/shard_map/all_gather | solution.py:33
  150.3 82.1 %all-gather.14.cloned.1.call-start = ((), (), s32[]{:S(2)}) async-start(), calls=%async_computation.5 | async-start | bytes 4718592 | tf_op jit(solution)/shard_map/all_gather | solution.py:33
  190.0 1.3 copy-start
  195.7 86.1 %all-gather.16.cloned.1.call-start = ((), (), s32[]{:S(2)}) async-start(), calls=%async_computation.6 | async-start | bytes 4718592 | tf_op jit(solution)/shard_map/all_gather | solution.py:33
  235.5 1.6 copy-start.1
  245.1 86.9 %all-gather.18.cloned.1.call-start = ((), (), s32[]{:S(2)}) async-start(), calls=%async_computation.7 | async-start | bytes 2359296 | tf_op jit(solution)/shard_map/all_gather | solution.py:85
  288.9 2.1 copy-start.4
Sparse Core Ops, SparseCore 0:
  11.3 43.8 reduce-scatter.1
  98.9 28.9 all-gather.9
  150.5 34.1 all-gather.11
  195.8 36.5 all-gather.13
  245.2 36.5 all-gather.15
  291.2 28.1 all-gather.17
